TPU v7x, 128 devices: a whole 4x4x4 slice. The times are simulated.
128 devices in a mesh: band: 8 (over z, core), chan: 16 (over x, y).
Axes of the slice: x: 4, y: 4, z: 4, core: 2. Of those that a mesh axis runs over, the one named last changes fastest.
Arguments:
- voltages: bfloat16 [128, 2, 512, 2048], P('band', None, None, 'chan'), may hold values from -6 to 6
- weights: bfloat16 [128, 2, 2048, 2048], P(('band', 'chan')), may hold values from -0.125 to 0.125
- beam_order: int32 [2048], replicated, may hold values from 0 to 2047, each once
- delay_merge_tables: int32 [127, 64, 3], replicated, may hold values from 0 to 63, as said below
Outputs:
- fdmt_out: float32 [2048, 64, 128], P(('band', 'chan'))
Inputs may be any that keep to these rules, and one draw needn't show every extreme that they name: `beam_order`: each beam appears exactly once. `delay_merge_tables`: row 128 - (128 >> (l - 1)) + g is the node of level l (l = 1, ..., log2 128) that merges groups 2 g and 2 g + 1 of 2**(l - 1) adjacent channels each; for delays d < min(64, 2**(l + 1)) column 0 and column 1 are delays of the lower and the upper group, below the lower level's delay count (1 at level 1, else min(64, 2**l)), and column 2 is the time shift of the upper group, below min(64, 2**(l + 1)); the shifts of the used delays of one node are distinct; entries of larger delays are not read.
All inputs are finite; a program needn't handle non-finite values.
Results may differ from a plain program's by a relative error of at most 0.0003.
Values may be sent and summed in bfloat16 or wider, within the bound.
A program may use at most 128 MiB of HBM per device.

v0:
```python
import functools
import math

import jax
import jax.numpy as jnp
from jax import lax
from jax.experimental import pallas as pl
from jax.experimental.pallas import tpu as pltpu
from jax.sharding import PartitionSpec as P

MESH = pl.DeviceIdType.MESH
DELAYS = 64
SIDE = 4
CHANS = 16
BANDS = 8
CHANNELS = CHANS * BANDS
BLOCK = 16
AVG = 128
SAMPLES = 512
TILE = 256

STEPS = (
    (0, 0), (0, 2), (3, 0), (1, 2), (3, 3), (1, 1), (3, 1), (0, 3),
    (1, 3), (2, 1), (2, 3), (3, 2), (1, 0), (2, 2), (0, 1), (2, 0),
)


def beam_kernel(v_ref, w_ref, order_hbm, out_ref, xbuf, wbuf, nbuf, acc, pw, norm, send, order,
                x_send, x_recv, w_sem, o_sem, ready, s_sem, r_sem):
    band = lax.axis_index("band")
    chan = lax.axis_index("chan")
    x, y = chan // SIDE, lax.rem(chan, SIDE)
    beams = w_ref.shape[3]
    tiles = beams // TILE

    def ahead(step):
        return lax.rem(x + step[0], SIDE) * SIDE + lax.rem(y + step[1], SIDE)

    def behind(step):
        return lax.rem(x + SIDE - step[0], SIDE) * SIDE + lax.rem(y + SIDE - step[1], SIDE)

    barrier = pltpu.get_barrier_semaphore()
    for step in STEPS[1:]:
        pl.semaphore_signal(barrier, inc=1, device_id={"band": band, "chan": ahead(step)}, device_id_type=MESH)
    for k in range(1, BANDS):
        pl.semaphore_signal(barrier, inc=1, device_id={"band": lax.rem(band + k, BANDS), "chan": chan}, device_id_type=MESH)

    own = pltpu.make_async_copy(v_ref.at[chan], xbuf.at[0], x_recv.at[0])
    own.start()
    loads = []
    for k, step in enumerate(STEPS):
        rows = pl.ds(pl.multiple_of(behind(step) * 128, 128), 128)
        for part in range(2):
            load = pltpu.make_async_copy(w_ref.at[0, part, rows, :], wbuf.at[k, pl.ds(part * 128, 128), :], w_sem.at[k])
            load.start()
            loads.append(load)
    order_copy = pltpu.make_async_copy(order_hbm, order, o_sem)
    order_copy.start()

    pl.semaphore_wait(barrier, CHANS - 1 + BANDS - 1)
    copies = []
    for k, step in enumerate(STEPS):
        if k == 0:
            continue
        peer = ahead(step)
        copy = pltpu.make_async_remote_copy(
            v_ref.at[peer], xbuf.at[k], x_send.at[k], x_recv.at[k],
            device_id={"band": band, "chan": peer}, device_id_type=MESH)
        copy.start()
        copies.append(copy)
    for step in STEPS[1:]:
        pl.semaphore_signal(ready, inc=1, device_id={"band": band, "chan": ahead(step)}, device_id_type=MESH)

    def arrived(k, slot):
        pltpu.make_async_copy(xbuf.at[k], xbuf.at[k], x_recv.at[k]).wait()
        pltpu.make_async_copy(wbuf.at[k], wbuf.at[k], w_sem.at[k]).wait()
        nbuf[slot] = -xbuf[k, 1]

    def lhs_of(ks):
        top, low = [], []
        for slot, k in enumerate(ks):
            top += [xbuf[k, 0], nbuf[slot]]
            low += [xbuf[k, 1], xbuf[k, 0]]
        return jnp.concatenate([jnp.concatenate(top, axis=1), jnp.concatenate(low, axis=1)], axis=0)

    def columns(n):
        return pl.ds(pl.multiple_of(n * TILE, TILE), TILE)

    def pair(j, first):
        k = 2 * j
        arrived(k, 0)
        arrived(k + 1, 1)

        def one_tile(n, carry):
            rhs = wbuf[pl.ds(k, 2), :, columns(n)].reshape(512, TILE)
            got = jnp.dot(lhs_of((k, k + 1)), rhs, preferred_element_type=jnp.float32)
            if first:
                acc[n] = got
            else:
                acc[n] += got
            return carry

        lax.fori_loop(0, tiles, one_tile, 0)

    pair(0, True)

    def later(j, carry):
        pair(j, False)
        return carry

    lax.fori_loop(1, 7, later, 0)
    arrived(14, 0)

    def single(n, carry):
        acc[n] += jnp.dot(lhs_of((14,)), wbuf[14, :, columns(n)], preferred_element_type=jnp.float32)
        return carry

    lax.fori_loop(0, tiles, single, 0)
    arrived(15, 0)

    def final(n, carry):
        got = acc[n] + jnp.dot(lhs_of((15,)), wbuf[15, :, columns(n)], preferred_element_type=jnp.float32)
        real, imag = got[:SAMPLES], got[SAMPLES:]
        power = real * real + imag * imag
        for half in range(TILE // 128):
            pw[half] = power[:, half * 128 : (half + 1) * 128]
            total = pw[half, pl.ds(0, AVG, stride=4), :]
            for t in range(1, 4):
                total = total + pw[half, pl.ds(t, AVG, stride=4), :]
            mean4 = total * 0.25
            centered = mean4 - jnp.mean(mean4, axis=0, keepdims=True)
            spread = jnp.mean(centered * centered, axis=0, keepdims=True)
            scaled = centered * (1.0 / jnp.sqrt(spread + 1e-05))
            norm[pl.ds(pl.multiple_of(n * TILE + half * 128, 128), 128), :] = scaled.T
        return carry

    lax.fori_loop(0, tiles, final, 0)
    for copy in copies:
        copy.wait_send()

    order_copy.wait()
    pl.semaphore_wait(ready, CHANS - 1)
    me = band * CHANS + chan

    def gather(r, block):
        for i in range(BLOCK):
            send[r, pl.ds(i, 1), :] = norm[pl.ds(order[block * BLOCK + i], 1), :]

    def one_send(r, carry):
        to_band = lax.rem(band + r // CHANS, BANDS)
        rc = lax.rem(r, CHANS)
        to_chan = lax.rem(x + rc // SIDE, SIDE) * SIDE + lax.rem(y + rc, SIDE)
        gather(r, to_band * CHANS + to_chan)
        pltpu.make_async_remote_copy(
            send.at[r], out_ref.at[me], s_sem, r_sem,
            device_id={"band": to_band, "chan": to_chan}, device_id_type=MESH).start()
        return carry

    lax.fori_loop(1, CHANNELS, one_send, 0)
    gather(0, me)
    keep = pltpu.make_async_copy(send.at[0], out_ref.at[me], o_sem)
    keep.start()
    keep.wait()
    others = pl.ds(1, CHANNELS - 1)
    pltpu.make_async_copy(send.at[others], send.at[others], s_sem).wait()
    pltpu.make_async_copy(send.at[others], send.at[others], r_sem).wait()


def beamform(voltages, weights, beam_order):
    beams = weights.shape[3]
    any_space = pl.BlockSpec(memory_space=pl.ANY)
    return pl.pallas_call(
        beam_kernel,
        out_shape=jax.ShapeDtypeStruct((CHANNELS, BLOCK, AVG), jnp.float32),
        in_specs=[any_space] * 3,
        out_specs=pl.BlockSpec(memory_space=pltpu.VMEM),
        scratch_shapes=[
            pltpu.VMEM((CHANS, 2, SAMPLES, 128), jnp.bfloat16),
            pltpu.VMEM((CHANS, 256, beams), jnp.bfloat16),
            pltpu.VMEM((2, SAMPLES, 128), jnp.bfloat16),
            pltpu.VMEM((beams // TILE, 2 * SAMPLES, TILE), jnp.float32),
            pltpu.VMEM((TILE // 128, SAMPLES, 128), jnp.float32),
            pltpu.VMEM((beams, AVG), jnp.float32),
            pltpu.VMEM((CHANNELS, BLOCK, AVG), jnp.float32),
            pltpu.SMEM((beams,), jnp.int32),
            pltpu.SemaphoreType.DMA((CHANS,)),
            pltpu.SemaphoreType.DMA((CHANS,)),
            pltpu.SemaphoreType.DMA((CHANS,)),
            pltpu.SemaphoreType.DMA,
            pltpu.SemaphoreType.REGULAR,
            pltpu.SemaphoreType.DMA,
            pltpu.SemaphoreType.DMA,
        ],
        compiler_params=pltpu.CompilerParams(
            collective_id=0, has_side_effects=True, vmem_limit_bytes=56 * 2**20),
    )(voltages, weights, beam_order)


def merge_kernel(table, start, out_ref, even, odd):
    lanes = lax.broadcasted_iota(jnp.int32, (BLOCK, AVG), 1)
    levels = CHANNELS.bit_length() - 1
    source, before = start, 1
    for level in range(1, levels + 1):
        groups = CHANNELS >> level
        count = min(DELAYS, 2 ** (level + 1))
        first_row = CHANNELS - (CHANNELS >> (level - 1))
        target = out_ref if level == levels else (even if level % 2 == 0 else odd)
        unroll = min(count, 8)
        parts = count // unroll

        def step(i, carry, source=source, target=target, before=before, count=count, first_row=first_row,
                 unroll=unroll, parts=parts, level=level):
            g = i // parts
            d0 = lax.rem(i, parts) * unroll
            for u in range(unroll):
                d = d0 + u
                r = first_row + g
                shift = table[2, d, r]
                low_row, high_row = 2 * g * before, (2 * g + 1) * before
                if level > 1:
                    low_row = low_row + table[0, d, r]
                    high_row = high_row + table[1, d, r]
                moved = pltpu.roll(source[high_row], lax.rem(AVG - shift, AVG), 1)
                merged = source[low_row] + jnp.where(lanes < AVG - shift, moved, 0.0)
                if level == levels:
                    target[:, pl.ds(d, 1), :] = (merged * (1.0 / math.sqrt(CHANNELS))).reshape(BLOCK, 1, AVG)
                else:
                    target[g * count + d] = merged
            return carry

        lax.fori_loop(0, groups * parts, step, 0)
        source, before = target, count


def dedisperse(start, tables):
    return pl.pallas_call(
        merge_kernel,
        out_shape=jax.ShapeDtypeStruct((BLOCK, DELAYS, AVG), jnp.float32),
        in_specs=[pl.BlockSpec(memory_space=pltpu.SMEM), pl.BlockSpec(memory_space=pltpu.VMEM)],
        out_specs=pl.BlockSpec(memory_space=pltpu.VMEM),
        scratch_shapes=[
            pltpu.VMEM((256, BLOCK, AVG), jnp.float32),
            pltpu.VMEM((256, BLOCK, AVG), jnp.float32),
        ],
        compiler_params=pltpu.CompilerParams(vmem_limit_bytes=32 * 2**20),
    )(jnp.transpose(tables, (2, 1, 0)), start)


def body(voltages, weights, beam_order, delay_merge_tables):
    regrouped = beamform(voltages, weights, beam_order)
    return dedisperse(regrouped, delay_merge_tables)


def solution(mesh):
    return jax.shard_map(
        body,
        mesh=mesh,
        in_specs=(P("band", None, None, "chan"), P(("band", "chan"), None, None, None), P(), P()),
        out_specs=P(("band", "chan"), None, None),
        check_vma=False,
    )
```

profile of v0, /device:TPU:1, one launch (start us, length us, event | category | flops | bytes accessed | tf_op | source)
XLA Modules:
  0.0 118.0 jit_solution(1021715583448343221)
XLA Ops:
  0.0 0.0 copy-start.1
  0.0 92.7 %shard_map.46.start = f32[128,16,128]{2,1,0:T(8,128)} custom-call(bf16[16,2,512,128]{3,2,1,0:T(8,128)(2,1)} %v_ref.1, bf16[1,2,2048,2048]{3,2,1,0:T(8,128)(2,1)} %w_ref.1, s32[2048]{0:T(1024)} %order_hbm.1), custom_call_target="tpu_custom_call" | custom-call | tf_op jit(solution)/shard_map/pallas_call | solution.py:172
  92.7 0.0 copy-done.1
  92.7 0.0 copy-start
  92.7 1.2 %copy-done = f32[128,16,128]{2,1,0:T(8,128)S(1)} copy-done((f32[128,16,128]{2,1,0:T(8,128)S(1)}, f32[128,16,128]{2,1,0:T(8,128)}, u32[]{:S(2)}) %copy-start) | copy-done | bytes 1048600
  93.9 24.0 %shard_map.47 = f32[16,64,128]{2,1,0:T(8,128)} custom-call(s32[3,64,127]{2,1,0:T(8,128)S(1)} %bitcast.1, f32[128,16,128]{2,1,0:T(8,128)S(1)} %copy-done), custom_call_target="tpu_custom_call" | custom-call | tf_op jit(solution)/shard_map/pallas_call | solution.py:236
Async XLA Ops:
  0.0 92.7 %copy-start.1 = (s32[127,64,3]{0,1,2:T(8,128)S(1)}, s32[127,64,3]{0,1,2:T(8,128)}, u32[]{:S(2)}) copy-start(s32[127,64,3]{0,1,2:T(8,128)} %param.7) | copy-start | bytes 292612
  92.7 1.2 %copy-start = (f32[128,16,128]{2,1,0:T(8,128)S(1)}, f32[128,16,128]{2,1,0:T(8,128)}, u32[]{:S(2)}) copy-start(f32[128,16,128]{2,1,0:T(8,128)} %shard_map.46.start) | copy-start | bytes 3145732
where the time goes:
time: 118 us
  Pallas kernels  117 us (99%)
  local copies, waits for them, and re-layouts  1.22 us (1%)
    pallas_call x1, Pallas kernels, beamform(): pl.pallas_call(beam_kernel, out_shape=jax.ShapeDtypeStruct((CHANNELS, BLO...  92.7 us
    pallas_call x1, Pallas kernels, dedisperse(): pl.pallas_call(merge_kernel, out_shape=jax.ShapeDtypeStruct((BLOCK, DELAY...  24 us

commit v1 on v0

v1 whole, which is shorter than its diff:
```python
import functools
import math

import jax
import jax.numpy as jnp
from jax import lax
from jax.experimental import pallas as pl
from jax.experimental.pallas import tpu as pltpu
from jax.sharding import PartitionSpec as P

MESH = pl.DeviceIdType.MESH
DELAYS = 64
SIDE = 4
CHANS = 16
BANDS = 8
CHANNELS = CHANS * BANDS
LEVELS = CHANNELS.bit_length() - 1
INNER = CHANS.bit_length() - 1
BLOCK = 16
AVG = 128
CODE_TOP = 32760.0
STEPS_PER_OCTAVE = 16.0
FLOOR = 2.0**-100
SAMPLES = 512
TILE = 2048
LAST = 256

STEPS = (
    (0, 0), (0, 2), (3, 0), (1, 2), (3, 3), (1, 1), (3, 1), (0, 3),
    (1, 3), (2, 1), (2, 3), (3, 2), (1, 0), (2, 2), (0, 1), (2, 0),
)
ARRIVE = (
    (0, 0), (3, 0), (1, 2), (3, 3), (1, 1), (2, 1), (0, 2), (1, 3),
    (3, 1), (2, 3), (1, 0), (3, 2), (2, 2), (0, 3), (0, 1), (2, 0),
)


def counts(level):
    return 1 if level == 0 else min(DELAYS, 2 ** (level + 1))


def kernel(v_ref, w_ref, order_hbm, table_hbm, out_ref, xbuf, wbuf, nbuf, acc, pws, norm, stage, send, recv, order,
           raw, cooked, table, state1, state2, state3, state4, state5, state6,
           x_send, x_recv, w_sem, o_sem, t_sem, ready, s_sem, r_sem):
    band = lax.axis_index("band")
    chan = lax.axis_index("chan")
    x, y = chan // SIDE, lax.rem(chan, SIDE)
    beams = w_ref.shape[3]

    def ahead(step):
        return lax.rem(x + step[0], SIDE) * SIDE + lax.rem(y + step[1], SIDE)

    def behind(step):
        return lax.rem(x + SIDE - step[0], SIDE) * SIDE + lax.rem(y + SIDE - step[1], SIDE)

    barrier = pltpu.get_barrier_semaphore()
    for step in STEPS[1:]:
        pl.semaphore_signal(barrier, inc=1, device_id={"band": band, "chan": ahead(step)}, device_id_type=MESH)
    for k in range(1, BANDS):
        pl.semaphore_signal(barrier, inc=1, device_id={"band": lax.rem(band + k, BANDS), "chan": chan}, device_id_type=MESH)

    pltpu.make_async_copy(v_ref.at[chan], xbuf.at[0], x_recv.at[0]).start()
    for k, step in enumerate(ARRIVE):
        rows = pl.ds(pl.multiple_of(behind(step) * 128, 128), 128)
        for part in range(2):
            pltpu.make_async_copy(w_ref.at[0, part, rows, :], wbuf.at[k, pl.ds(part * 128, 128), :], w_sem.at[k]).start()
    order_copy = pltpu.make_async_copy(order_hbm, order, o_sem)
    order_copy.start()
    raw_copy = pltpu.make_async_copy(table_hbm, raw, t_sem)
    raw_copy.start()

    def clear(i, carry):
        acc[pl.ds(pl.multiple_of(i * 8, 8), 8), :] = jnp.zeros((8, beams), jnp.float32)
        return carry

    lax.fori_loop(0, 2 * SAMPLES // 8, clear, 0)
    pl.semaphore_wait(barrier, CHANS - 1 + BANDS - 1)
    copies = []
    for step in STEPS[1:]:
        k = ARRIVE.index(step)
        peer = ahead(step)
        copy = pltpu.make_async_remote_copy(
            v_ref.at[peer], xbuf.at[k], x_send.at[k], x_recv.at[k],
            device_id={"band": band, "chan": peer}, device_id_type=MESH)
        copy.start()
        copies.append(copy)
    for step in STEPS[1:]:
        pl.semaphore_signal(ready, inc=1, device_id={"band": band, "chan": ahead(step)}, device_id_type=MESH)

    raw_copy.wait()
    node = lax.broadcasted_iota(jnp.int32, (DELAYS, CHANNELS - 1), 1)
    low_base = jnp.zeros((DELAYS, CHANNELS - 1), jnp.int32)
    high_base = low_base
    for level in range(1, LEVELS + 1):
        first = CHANNELS - (CHANNELS >> (level - 1))
        group = node - first
        if level <= INNER:
            group = lax.rem(group, CHANS >> level)
        low_base = jnp.where(node >= first, 2 * group * counts(level - 1), low_base)
        high_base = jnp.where(node >= first, (2 * group + 1) * counts(level - 1), high_base)
    cooked[0] = raw[0] + low_base
    cooked[1] = raw[1] + high_base
    cooked[2] = AVG - raw[2]

    def arrived(k):
        pltpu.make_async_copy(xbuf.at[k], xbuf.at[k], x_recv.at[k]).wait()
        pltpu.make_async_copy(wbuf.at[k], wbuf.at[k], w_sem.at[k]).wait()
        nbuf[...] = -xbuf[k, 1]

    def product(k, cols):
        top = jnp.concatenate([xbuf[k, 0], nbuf[...]], axis=1)
        low = jnp.concatenate([xbuf[k, 1], xbuf[k, 0]], axis=1)
        return jnp.dot(jnp.concatenate([top, low], axis=0), wbuf[k, :, cols], preferred_element_type=jnp.float32)

    def columns(n, width):
        return slice(n * width, (n + 1) * width)

    def block(k):
        arrived(k)

        for n in range(beams // TILE):
            cols = columns(n, TILE)
            acc[:, cols] += product(k, cols)

    table_copy = pltpu.make_async_copy(cooked, table, t_sem)
    table_copy.start()

    def later(k, carry):
        block(k)
        return carry

    lax.fori_loop(0, CHANS - 1, later, 0)
    arrived(CHANS - 1)

    def final(n):
        cols = columns(n, LAST)
        got = acc[:, cols] + product(CHANS - 1, cols)
        real, imag = got[:SAMPLES], got[SAMPLES:]
        power = real * real + imag * imag
        for half in range(LAST // 128):
            pw = pws.at[n % 2]
            pw[half] = power[:, half * 128 : (half + 1) * 128]
            total = pw[half, pl.ds(0, AVG, stride=4), :]
            for t in range(1, 4):
                total = total + pw[half, pl.ds(t, AVG, stride=4), :]
            mean4 = total * 0.25
            centered = mean4 - jnp.mean(mean4, axis=0, keepdims=True)
            centered = centered - jnp.mean(centered, axis=0, keepdims=True)
            spread = jnp.mean(centered * centered, axis=0, keepdims=True)
            inverse = 1.0 / jnp.sqrt(spread + 1e-05)
            top = jnp.max(jnp.abs(centered), axis=0, keepdims=True) * inverse
            code = jnp.ceil(jnp.log2(jnp.maximum(top, FLOOR)) * STEPS_PER_OCTAVE)
            grow = inverse * (CODE_TOP * jnp.exp2(code * (-1.0 / STEPS_PER_OCTAVE)))
            whole = jnp.round(centered * grow)
            times = lax.broadcasted_iota(jnp.int32, whole.shape, 0)
            scaled = jnp.where(times == AVG - 1, code, whole)
            at = n * LAST + half * 128
            norm[at : at + 128, :] = scaled.T

    for n in range(beams // LAST):
        final(n)
    for copy in copies:
        copy.wait_send()

    order_copy.wait()
    table_copy.wait()
    pl.semaphore_wait(ready, CHANS - 1)
    me = band * CHANS + chan

    def gather(slot, at, block):
        for i in range(BLOCK):
            stage[at, pl.ds(i, 1), :] = norm[pl.ds(order[block * BLOCK + i], 1), :]
        send[slot] = stage[at].astype(jnp.int32).astype(jnp.int16)

    to_chans = [ahead((rc // SIDE, rc % SIDE)) for rc in range(CHANS)]

    def send_some(j, carry):
        to_band = lax.rem(band + j, BANDS)
        for i in range(CHANS):
            slot = j * CHANS + i

            def one(slot=slot, i=i):
                gather(slot, i, to_band * CHANS + to_chans[i])
                pltpu.make_async_remote_copy(
                    send.at[slot], recv.at[me], s_sem, r_sem.at[band],
                    device_id={"band": to_band, "chan": to_chans[i]}, device_id_type=MESH).start()

            if i == 0:
                pl.when(j > 0)(one)
            else:
                one()
        return carry

    lax.fori_loop(0, BANDS, send_some, 0)
    gather(CHANNELS, 0, me)
    pltpu.make_async_copy(send.at[CHANNELS], recv.at[me], r_sem.at[band]).start()

    lanes = lax.broadcasted_iota(jnp.int32, (BLOCK, AVG), 1)

    def shifted(high, keep):
        return jnp.where(lanes < keep, pltpu.roll(high, keep, 1), 0.0)

    def merge(r, count, source, store):
        for d in range(count):
            low = source[table[0, d, r]]
            store(d, low + shifted(source[table[1, d, r]], table[2, d, r]))

    def decoded(channel):
        got = recv[channel].astype(jnp.int32).astype(jnp.float32)
        last = lanes == AVG - 1
        code = jnp.sum(jnp.where(last, got, 0.0), axis=1, keepdims=True)
        got = jnp.where(last, 0.0, got)
        got = got - jnp.where(last, jnp.sum(got, axis=1, keepdims=True), 0.0)
        return got * (jnp.exp2(code * (1.0 / STEPS_PER_OCTAVE)) * (1.0 / CODE_TOP))

    def one_band(k, carry):
        q = lax.rem(band + BANDS - k, BANDS)
        got = recv.at[pl.ds(q * CHANS, CHANS)]
        pltpu.make_async_copy(got, got, r_sem.at[q]).wait()
        for i in range(CHANS // 2):
            low = decoded(q * CHANS + 2 * i)
            high = decoded(q * CHANS + 2 * i + 1)
            for d in range(4):
                state1[i * 4 + d] = low + shifted(high, table[2, d, q * 8 + i])
        for i in range(4):
            def store2(d, merged, i=i):
                state2[i * 8 + d] = merged
            merge(64 + q * 4 + i, 8, state1, store2)
        for i in range(2):
            def store3(d, merged, i=i):
                state3[i * 16 + d] = merged
            merge(96 + q * 2 + i, 16, state2, store3)

        def store4(d, merged):
            state4[q * 32 + d] = merged
        merge(112 + q, 32, state3, store4)
        return carry

    lax.fori_loop(0, BANDS, one_band, 0)
    for g in range(4):
        def store5(d, merged, g=g):
            state5[g * DELAYS + d] = merged
        merge(120 + g, DELAYS, state4, store5)
    for g in range(2):
        def store6(d, merged, g=g):
            state6[g * DELAYS + d] = merged
        merge(124 + g, DELAYS, state5, store6)

    def store7(d, merged):
        out_ref[d] = merged * (1.0 / math.sqrt(CHANNELS))
    merge(126, DELAYS, state6, store7)
    others = pl.ds(0, CHANNELS - 1)
    pltpu.make_async_copy(send.at[others], send.at[others], s_sem).wait()


def body(voltages, weights, beam_order, delay_merge_tables):
    beams = weights.shape[3]
    any_space = pl.BlockSpec(memory_space=pl.ANY)
    few = (32, BLOCK, AVG)
    got = pl.pallas_call(
        kernel,
        out_shape=jax.ShapeDtypeStruct((DELAYS, BLOCK, AVG), jnp.float32),
        in_specs=[any_space] * 4,
        out_specs=pl.BlockSpec(memory_space=pltpu.VMEM),
        scratch_shapes=[
            pltpu.VMEM((CHANS, 2, SAMPLES, 128), jnp.bfloat16),
            pltpu.VMEM((CHANS, 256, beams), jnp.bfloat16),
            pltpu.VMEM((SAMPLES, 128), jnp.bfloat16),
            pltpu.VMEM((2 * SAMPLES, beams), jnp.float32),
            pltpu.VMEM((2, LAST // 128, SAMPLES, 128), jnp.float32),
            pltpu.VMEM((beams, AVG), jnp.float32),
            pltpu.VMEM((CHANS, BLOCK, AVG), jnp.float32),
            pltpu.VMEM((CHANNELS + 1, BLOCK, AVG), jnp.int16),
            pltpu.VMEM((CHANNELS, BLOCK, AVG), jnp.int16),
            pltpu.SMEM((beams,), jnp.int32),
            pltpu.VMEM((3, DELAYS, CHANNELS - 1), jnp.int32),
            pltpu.VMEM((3, DELAYS, CHANNELS - 1), jnp.int32),
            pltpu.SMEM((3, DELAYS, CHANNELS - 1), jnp.int32),
            pltpu.VMEM(few, jnp.float32),
            pltpu.VMEM(few, jnp.float32),
            pltpu.VMEM(few, jnp.float32),
            pltpu.VMEM((256, BLOCK, AVG), jnp.float32),
            pltpu.VMEM((256, BLOCK, AVG), jnp.float32),
            pltpu.VMEM((128, BLOCK, AVG), jnp.float32),
            pltpu.SemaphoreType.DMA((CHANS,)),
            pltpu.SemaphoreType.DMA((CHANS,)),
            pltpu.SemaphoreType.DMA((CHANS,)),
            pltpu.SemaphoreType.DMA,
            pltpu.SemaphoreType.DMA,
            pltpu.SemaphoreType.REGULAR,
            pltpu.SemaphoreType.DMA,
            pltpu.SemaphoreType.DMA((BANDS,)),
        ],
        compiler_params=pltpu.CompilerParams(
            collective_id=0, has_side_effects=True, vmem_limit_bytes=56 * 2**20),
    )(voltages, weights, beam_order, jnp.transpose(delay_merge_tables, (2, 1, 0)))
    return jnp.transpose(got, (1, 0, 2))


def solution(mesh):
    return jax.shard_map(
        body,
        mesh=mesh,
        in_specs=(P("band", None, None, "chan"), P(("band", "chan"), None, None, None), P(), P()),
        out_specs=P(("band", "chan"), None, None),
        check_vma=False,
    )
```

time: 118 us -> 79.9 us (0.68)
  Pallas kernels: 117 us -> 77.7 us
    pallas_call x2 -> x1, Pallas kernels: 117 us -> 77.7 us  [body(): pl.pallas_call(kernel, out_shape=jax.ShapeDtypeStruct((DELAYS, BLOCK, AVG...]
    transpose x0 -> x1, local copies, waits for them, and re-layouts: none -> 2.01 us  [body(): return jnp.transpose(got, (1, 0, 2))]
    unnamed x4 -> x0, local copies, waits for them, and re-layouts: 1.22 us -> none
where the time goes in v1:
time: 79.9 us; the launch traced here: 79.7 us
  Pallas kernels  77.7 us (97%)
  local copies, waits for them, and re-layouts  2.01 us (3%)
    pallas_call x1, Pallas kernels, body(): pl.pallas_call(kernel, out_shape=jax.ShapeDtypeStruct((DELAYS, BLOCK, AVG...  77.7 us
    transpose x1, local copies, waits for them, and re-layouts, body(): return jnp.transpose(got, (1, 0, 2))  2.01 us

profile of v1, /device:TPU:1, one launch (start us, length us, event | category | flops | bytes accessed | tf_op | source)
XLA Modules:
  0.0 79.7 jit_solution(1223125784626398347)
XLA Ops:
  0.0 77.7 %shard_map.46 = f32[64,16,128]{2,1,0:T(8,128)} custom-call(bf16[16,2,512,128]{3,2,1,0:T(8,128)(2,1)} %v_ref.1, bf16[1,2,2048,2048]{3,2,1,0:T(8,128)(2,1)} %w_ref.1, s32[2048]{0:T(1024)} %order_hbm.1, s32[3,64,127]{2,1,0:T(8,128)} %bitcast.3), custom_call_target="tpu_custom_call" | custom-call | tf_op jit(solution)/shard_map/pallas_call | solution.py:260
  77.7 2.0 %copy.5 = f32[16,64,128]{2,1,0:T(8,128)} copy(f32[16,64,128]{2,0,1:T(8,128)} %bitcast.2) | data formatting | bytes 1048576 | tf_op jit(solution)/shard_map/transpose | solution.py:297

commit v2 on v1

--- a/solution.py
+++ b/solution.py
@@ -15,7 +15,6 @@
 BANDS = 8
 CHANNELS = CHANS * BANDS
 LEVELS = CHANNELS.bit_length() - 1
-INNER = CHANS.bit_length() - 1
 BLOCK = 16
 AVG = 128
 CODE_TOP = 32760.0
@@ -33,6 +32,12 @@
     (0, 0), (3, 0), (1, 2), (3, 3), (1, 1), (2, 1), (0, 2), (1, 3),
     (3, 1), (2, 3), (1, 0), (3, 2), (2, 2), (0, 3), (0, 1), (2, 0),
 )
+
+FAR = (
+    (2, 2), (2, 1), (1, 2), (2, 3), (3, 2), (1, 1), (3, 3), (1, 3),
+    (3, 1), (2, 0), (0, 2), (1, 0), (0, 1), (3, 0), (0, 3), (0, 0),
+)
+SLOTS = tuple((i + 1) % CHANS for i in range(CHANS))
 
 
 def counts(level):
@@ -94,8 +99,6 @@
     for level in range(1, LEVELS + 1):
         first = CHANNELS - (CHANNELS >> (level - 1))
         group = node - first
-        if level <= INNER:
-            group = lax.rem(group, CHANS >> level)
         low_base = jnp.where(node >= first, 2 * group * counts(level - 1), low_base)
         high_base = jnp.where(node >= first, (2 * group + 1) * counts(level - 1), high_base)
     cooked[0] = raw[0] + low_base
@@ -134,12 +137,13 @@
 
     def final(n):
         cols = columns(n, LAST)
+        pw = pws.at[n % 2]
         got = acc[:, cols] + product(CHANS - 1, cols)
         real, imag = got[:SAMPLES], got[SAMPLES:]
         power = real * real + imag * imag
         for half in range(LAST // 128):
-            pw = pws.at[n % 2]
             pw[half] = power[:, half * 128 : (half + 1) * 128]
+        for half in range(LAST // 128):
             total = pw[half, pl.ds(0, AVG, stride=4), :]
             for t in range(1, 4):
                 total = total + pw[half, pl.ds(t, AVG, stride=4), :]
@@ -172,12 +176,12 @@
             stage[at, pl.ds(i, 1), :] = norm[pl.ds(order[block * BLOCK + i], 1), :]
         send[slot] = stage[at].astype(jnp.int32).astype(jnp.int16)
 
-    to_chans = [ahead((rc // SIDE, rc % SIDE)) for rc in range(CHANS)]
+    to_chans = [ahead(step) for step in FAR]
 
     def send_some(j, carry):
         to_band = lax.rem(band + j, BANDS)
         for i in range(CHANS):
-            slot = j * CHANS + i
+            slot = j * CHANS + SLOTS[i]
 
             def one(slot=slot, i=i):
                 gather(slot, i, to_band * CHANS + to_chans[i])
@@ -185,25 +189,20 @@
                     send.at[slot], recv.at[me], s_sem, r_sem.at[band],
                     device_id={"band": to_band, "chan": to_chans[i]}, device_id_type=MESH).start()
 
-            if i == 0:
+            if FAR[i] == (0, 0):
                 pl.when(j > 0)(one)
             else:
                 one()
         return carry
 
     lax.fori_loop(0, BANDS, send_some, 0)
-    gather(CHANNELS, 0, me)
-    pltpu.make_async_copy(send.at[CHANNELS], recv.at[me], r_sem.at[band]).start()
+    gather(0, 0, me)
+    pltpu.make_async_copy(send.at[0], recv.at[me], r_sem.at[band]).start()
 
     lanes = lax.broadcasted_iota(jnp.int32, (BLOCK, AVG), 1)
 
     def shifted(high, keep):
         return jnp.where(lanes < keep, pltpu.roll(high, keep, 1), 0.0)
-
-    def merge(r, count, source, store):
-        for d in range(count):
-            low = source[table[0, d, r]]
-            store(d, low + shifted(source[table[1, d, r]], table[2, d, r]))
 
     def decoded(channel):
         got = recv[channel].astype(jnp.int32).astype(jnp.float32)
@@ -213,53 +212,45 @@
         got = got - jnp.where(last, jnp.sum(got, axis=1, keepdims=True), 0.0)
         return got * (jnp.exp2(code * (1.0 / STEPS_PER_OCTAVE)) * (1.0 / CODE_TOP))
 
-    def one_band(k, carry):
-        q = lax.rem(band + BANDS - k, BANDS)
+    def one_band(j, carry):
+        q = lax.rem(band + BANDS - j, BANDS)
         got = recv.at[pl.ds(q * CHANS, CHANS)]
         pltpu.make_async_copy(got, got, r_sem.at[q]).wait()
         for i in range(CHANS // 2):
             low = decoded(q * CHANS + 2 * i)
             high = decoded(q * CHANS + 2 * i + 1)
             for d in range(4):
-                state1[i * 4 + d] = low + shifted(high, table[2, d, q * 8 + i])
-        for i in range(4):
-            def store2(d, merged, i=i):
-                state2[i * 8 + d] = merged
-            merge(64 + q * 4 + i, 8, state1, store2)
-        for i in range(2):
-            def store3(d, merged, i=i):
-                state3[i * 16 + d] = merged
-            merge(96 + q * 2 + i, 16, state2, store3)
-
-        def store4(d, merged):
-            state4[q * 32 + d] = merged
-        merge(112 + q, 32, state3, store4)
+                state1[q * 32 + i * 4 + d] = low + shifted(high, table[2, d, q * 8 + i])
         return carry
 
     lax.fori_loop(0, BANDS, one_band, 0)
-    for g in range(4):
-        def store5(d, merged, g=g):
-            state5[g * DELAYS + d] = merged
-        merge(120 + g, DELAYS, state4, store5)
-    for g in range(2):
-        def store6(d, merged, g=g):
-            state6[g * DELAYS + d] = merged
-        merge(124 + g, DELAYS, state5, store6)
-
-    def store7(d, merged):
-        out_ref[d] = merged * (1.0 / math.sqrt(CHANNELS))
-    merge(126, DELAYS, state6, store7)
-    others = pl.ds(0, CHANNELS - 1)
+
+    def merge(level, source, target):
+        count = counts(level)
+        for g in range(CHANNELS >> level):
+            r = CHANNELS - (CHANNELS >> (level - 1)) + g
+            for d in range(count):
+                low = source[table[0, d, r]]
+                merged = low + shifted(source[table[1, d, r]], table[2, d, r])
+                if level == LEVELS:
+                    target[pl.ds(d, BLOCK, stride=DELAYS), :] = merged
+                else:
+                    target[g * count + d] = merged
+
+    states = (None, state1, state2, state3, state4, state5, state6, out_ref)
+    for level in range(2, LEVELS + 1):
+        merge(level, states[level - 1], states[level])
+    others = pl.ds(1, CHANNELS - 1)
     pltpu.make_async_copy(send.at[others], send.at[others], s_sem).wait()
 
 
 def body(voltages, weights, beam_order, delay_merge_tables):
     beams = weights.shape[3]
     any_space = pl.BlockSpec(memory_space=pl.ANY)
-    few = (32, BLOCK, AVG)
+    whole = (256, BLOCK, AVG)
     got = pl.pallas_call(
         kernel,
-        out_shape=jax.ShapeDtypeStruct((DELAYS, BLOCK, AVG), jnp.float32),
+        out_shape=jax.ShapeDtypeStruct((BLOCK * DELAYS, AVG), jnp.float32),
         in_specs=[any_space] * 4,
         out_specs=pl.BlockSpec(memory_space=pltpu.VMEM),
         scratch_shapes=[
@@ -270,15 +261,15 @@
             pltpu.VMEM((2, LAST // 128, SAMPLES, 128), jnp.float32),
             pltpu.VMEM((beams, AVG), jnp.float32),
             pltpu.VMEM((CHANS, BLOCK, AVG), jnp.float32),
-            pltpu.VMEM((CHANNELS + 1, BLOCK, AVG), jnp.int16),
+            pltpu.VMEM((CHANNELS, BLOCK, AVG), jnp.int16),
             pltpu.VMEM((CHANNELS, BLOCK, AVG), jnp.int16),
             pltpu.SMEM((beams,), jnp.int32),
             pltpu.VMEM((3, DELAYS, CHANNELS - 1), jnp.int32),
             pltpu.VMEM((3, DELAYS, CHANNELS - 1), jnp.int32),
             pltpu.SMEM((3, DELAYS, CHANNELS - 1), jnp.int32),
-            pltpu.VMEM(few, jnp.float32),
-            pltpu.VMEM(few, jnp.float32),
-            pltpu.VMEM(few, jnp.float32),
+            pltpu.VMEM(whole, jnp.float32),
+            pltpu.VMEM(whole, jnp.float32),
+            pltpu.VMEM(whole, jnp.float32),
             pltpu.VMEM((256, BLOCK, AVG), jnp.float32),
             pltpu.VMEM((256, BLOCK, AVG), jnp.float32),
             pltpu.VMEM((128, BLOCK, AVG), jnp.float32),
@@ -292,9 +283,9 @@
             pltpu.SemaphoreType.DMA((BANDS,)),
         ],
         compiler_params=pltpu.CompilerParams(
-            collective_id=0, has_side_effects=True, vmem_limit_bytes=56 * 2**20),
+            collective_id=0, has_side_effects=True, vmem_limit_bytes=52 * 2**20),
     )(voltages, weights, beam_order, jnp.transpose(delay_merge_tables, (2, 1, 0)))
-    return jnp.transpose(got, (1, 0, 2))
+    return got.reshape(BLOCK, DELAYS, AVG) * (1.0 / math.sqrt(CHANNELS))
 
 
 def solution(mesh):

time: 79.9 us -> 78.4 us (0.981)
  Pallas kernels: 77.7 us -> 75.8 us
  other arithmetic: 0 us -> 0.84 us
    transpose x1 -> x0, local copies, waits for them, and re-layouts: 2.01 us -> none  [body(): return jnp.transpose(got, (1, 0, 2))]
    pallas_call x1, Pallas kernels: 77.7 us -> 75.8 us  [body(): pl.pallas_call(kernel, out_shape=jax.ShapeDtypeStruct((BLOCK * DELAYS, AV...]
    unnamed x0 -> x4, local copies, waits for them, and re-layouts: none -> 1.59 us
    mul x0 -> x1, other arithmetic: none -> 0.84 us  [body(): return got.reshape(BLOCK, DELAYS, AVG) * (1.0 / math.sqrt(CHANNELS))]
where the time goes in v2:
time: 78.4 us; the launch traced here: 78.3 us
  Pallas kernels  75.8 us (97%)
  local copies, waits for them, and re-layouts  1.59 us (2%)
  other arithmetic  0.84 us (1%)
    pallas_call x1, Pallas kernels, body(): pl.pallas_call(kernel, out_shape=jax.ShapeDtypeStruct((BLOCK * DELAYS, AV...  75.8 us
    unnamed x4, local copies, waits for them, and re-layouts  1.59 us

profile of v2, /device:TPU:1, one launch (start us, length us, event | category | flops | bytes accessed | tf_op | source)
XLA Modules:
  0.0 78.3 jit_solution(1885672479692415377)
XLA Ops:
  0.0 0.0 copy-start
  0.0 0.9 %copy-done = s32[127,64,3]{0,1,2:T(8,128)S(1)} copy-done((s32[127,64,3]{0,1,2:T(8,128)S(1)}, s32[127,64,3]{0,1,2:T(8,128)}, u32[]{:S(2)}) %copy-start) | copy-done | bytes 97560
  0.9 0.0 copy-start.1
  0.9 0.7 copy-done.1
  1.6 75.8 %shard_map.46 = f32[1024,128]{1,0:T(8,128)S(1)} custom-call(bf16[16,2,512,128]{3,2,1,0:T(8,128)(2,1)} %v_ref.1, bf16[1,2,2048,2048]{3,2,1,0:T(8,128)(2,1)} %w_ref.1, s32[2048]{0:T(1024)S(1)} %copy-done.1, s32[3,64,127]{2,1,0:T(8,128)S(1)} %bitcast.2), custom_call_target="tpu_custom_call" | custom-call | tf_op jit(solution)/shard_map/pallas_call | solution.py:251
  77.4 0.8 %broadcast_multiply_fusion = f32[1024,128]{1,0:T(8,128)} fusion(f32[1024,128]{1,0:T(8,128)S(1)} %shard_map.46), kind=kLoop, calls=%fused_computation | loop fusion | flops 131072 | bytes 1048576 | tf_op jit(solution)/shard_map/mul | solution.py:288
Async XLA Ops:
  0.0 0.9 %copy-start = (s32[127,64,3]{0,1,2:T(8,128)S(1)}, s32[127,64,3]{0,1,2:T(8,128)}, u32[]{:S(2)}) copy-start(s32[127,64,3]{0,1,2:T(8,128)} %param.7) | copy-start | bytes 292612
  0.9 0.7 copy-start.1
